TPU v7x, 32 devices: a whole 2x2x4 slice. The times are simulated.
32 devices in a mesh: sky: 2 (over x), tm: 16 (over z, y, core).
Axes of the slice: x: 2, y: 2, z: 4, core: 2. Of those that a mesh axis runs over, the one named last changes fastest.
Arguments:
- series: bfloat16 [4, 4, 1024, 2048], P('sky', None, 'tm'), parts along dimension 0, may hold values from -6 to 6
- antenna: float32 [4, 3], P('sky'), parts along dimension 0, as said below
- offsets: int32 [16, 2], P('sky'), parts along dimension 0, may hold values from -8 to 8, as said below
Outputs:
- detection: float32 [16, 1024, 2048], P('sky', 'tm'), parts along dimension 0
There are 2 independent parts, one for each index of `sky`. A program takes and returns all parts, laid end to end along the dimension named above; each array names one. Nothing has to cross between parts.
Inputs may be any that keep to these rules, and one draw needn't show every extreme that they name: `offsets`: both -8 and 8 occur in every draw. `antenna`: A and B are positive and C C is at most 0.49 A B in every row.
All inputs are finite; a program needn't handle non-finite values.
Results may differ from a plain program's by a relative error of at most 0.0032.
Values may be sent and summed in bfloat16 or wider, within the bound.
A program may use at most 128 MiB of HBM per device.

v0:
```python
import math

import jax
import jax.numpy as jnp
from jax import lax
from jax.sharding import PartitionSpec as P

NA = 2048
NB = 1024
LEN = 2097152
DMAX = 8


def with_halo(cells, sides, width):
    for axis, dim in sides:
        count = lax.axis_size(axis)
        head = lax.slice_in_dim(cells, 0, width, axis=dim)
        tail = lax.slice_in_dim(cells, cells.shape[dim] - width, cells.shape[dim], axis=dim)
        cells = jnp.concatenate(
            [
                lax.ppermute(tail, axis, [(i, (i + 1) % count) for i in range(count)]),
                cells,
                lax.ppermute(head, axis, [((i + 1) % count, i) for i in range(count)]),
            ],
            axis=dim,
        )
    return cells


def dft_table(length):
    indices = jnp.arange(length, dtype=jnp.int32)
    products = indices[:, None] * indices[None, :] % length
    phase_angle = products.astype(jnp.float32) * (2.0 * math.pi / length)
    return (jnp.cos(phase_angle).astype(jnp.bfloat16), (-jnp.sin(phase_angle)).astype(jnp.bfloat16))


def complex_dft(x_real, x_imag, w_real, w_imag, formula):
    real_part = jnp.einsum(
        formula, x_real, w_real, preferred_element_type=jnp.float32
    ) - jnp.einsum(formula, x_imag, w_imag, preferred_element_type=jnp.float32)
    imag_part = jnp.einsum(
        formula, x_real, w_imag, preferred_element_type=jnp.float32
    ) + jnp.einsum(formula, x_imag, w_real, preferred_element_type=jnp.float32)
    return (real_part, imag_part)


def projection(spectra, antenna):
    coef_a = antenna[:, 0][:, None, None]
    coef_b = antenna[:, 1][:, None, None]
    coef_c = antenna[:, 2][:, None, None]
    a_real, a_imag, b_real, b_imag = (spectra[:, 0], spectra[:, 1], spectra[:, 2], spectra[:, 3])
    numer = (
        coef_b * (a_real * a_real + a_imag * a_imag)
        + coef_a * (b_real * b_real + b_imag * b_imag)
        - 2.0 * coef_c * (a_real * b_real + a_imag * b_imag)
    )
    return numer / ((coef_a * coef_b - coef_c * coef_c) * LEN)


def carry_rims(widened, my_index, group_size):
    lower_rim = widened[..., :DMAX, :]
    upper_rim = widened[..., widened.shape[-2] - DMAX :, :]
    middle = widened[..., DMAX : widened.shape[-2] - DMAX, :]
    lower_rim = jnp.where(my_index == 0, jnp.roll(lower_rim, 1, axis=-1), lower_rim)
    upper_rim = jnp.where(my_index == group_size - 1, jnp.roll(upper_rim, -1, axis=-1), upper_rim)
    return jnp.concatenate([lower_rim, middle, upper_rim], axis=-2)


def local(series, antenna, offsets):
    group_size = lax.axis_size("tm")
    my_index = lax.axis_index("tm")
    seg_count = series.shape[0]
    col_block = NA // group_size
    row_block = NB // group_size
    short_real, short_imag = dft_table(NB)
    long_real, long_imag = dft_table(NA)
    columns = my_index * col_block + jnp.arange(col_block, dtype=jnp.int32)
    bins = jnp.arange(NB, dtype=jnp.int32)
    twist = (columns[:, None] * bins[None, :] % LEN).astype(jnp.float32) * (2.0 * math.pi / LEN)
    twid_real = jnp.cos(twist)
    twid_imag = -jnp.sin(twist)
    members = lax.all_to_all(series, "tm", split_axis=3, concat_axis=2, tiled=True)
    pieces = []
    for lead in (0, 2):
        real_part, imag_part = complex_dft(
            members[:, lead], members[:, lead + 1], short_real, short_imag, "snj,nk->sjk"
        )
        pieces.append((real_part * twid_real - imag_part * twid_imag).astype(jnp.bfloat16))
        pieces.append((real_part * twid_imag + imag_part * twid_real).astype(jnp.bfloat16))
    twiddled = jnp.stack(pieces, axis=1)
    members = lax.all_to_all(twiddled, "tm", split_axis=3, concat_axis=2, tiled=True)
    pieces = []
    for lead in (0, 2):
        real_part, imag_part = complex_dft(
            members[:, lead], members[:, lead + 1], long_real, long_imag, "sjk,jm->skm"
        )
        pieces.append(real_part)
        pieces.append(imag_part)
    spectra = jnp.stack(pieces, axis=1)
    local_fstat = projection(spectra, antenna)
    widened = with_halo(local_fstat, (("tm", 1),), DMAX)
    fstat = carry_rims(widened, my_index, group_size)

    def one_template(shift_row):
        total_sum = jnp.zeros((row_block, fstat.shape[-1]), jnp.float32)
        for segment in range(seg_count):
            total_sum = total_sum + lax.dynamic_slice_in_dim(
                fstat[segment], DMAX + shift_row[segment], row_block, 0
            )
        return total_sum / seg_count

    return jax.vmap(one_template)(offsets)


def solution(mesh):
    return jax.shard_map(
        local,
        mesh=mesh,
        in_specs=(P("sky", None, "tm", None), P("sky", None), P("sky", None)),
        out_specs=P("sky", "tm", None),
        check_vma=False,
    )
```

profile of v0, /device:TPU:0, one launch (start us, length us, event | category | flops | bytes accessed | tf_op | source)
XLA Modules:
  0.0 823.0 jit_solution(13590699504067278023)
XLA Ops:
  0.0 7.0 copy.6
  7.0 7.5 reshape.137
  14.5 7.4 all-to-all-start
  24.0 38.9 %all-to-all-done = bf16[16,2,32768]{2,1,0:T(2,128)(2,1)S(1)} async-done(((bf16[16,2,32768]{2,1,0:T(2,128)(2,1)}), bf16[16,2,32768]{2,1,0:T(2,128)(2,1)S(1)}, u32[]{:S(2)}, u32[]{:S(2)}) %all-to-all-start) | async-done | bytes 2097184 | tf_op jit(solution)/shard_map/all_to_all | solution.py:82
  62.9 4.9 reshape.138
  67.8 6.0 copy.7
  73.8 16.2 %fusion.44 = f32[1024,2,128]{2,0,1:T(8,128)S(1)} fusion(bf16[2,4,1024,128]{3,2,0,1:T(8,128)(2,1)S(1)} %bitcast.189), kind=kOutput, calls=%fused_computation.45 | convolution fusion | flops 553648128 | bytes 1572864 | tf_op jit(solution)/shard_map/snj,nk->sjk/dot_general | solution.py:41
  90.0 16.0 %fusion.48 = f32[1024,2,128]{2,0,1:T(8,128)S(1)} fusion(bf16[2,4,1024,128]{3,2,0,1:T(8,128)(2,1)S(1)} %bitcast.190), kind=kOutput, calls=%fused_computation.47 | convolution fusion | flops 553648128 | bytes 1572864 | tf_op jit(solution)/shard_map/snj,nk->sjk/dot_general | solution.py:41
  106.1 16.5 %fusion.46 = f32[1024,2,128]{2,0,1:T(8,128)S(1)} fusion(bf16[2,4,1024,128]{3,2,0,1:T(8,128)(2,1)S(1)} %bitcast.191), kind=kOutput, calls=%fused_computation.46 | convolution fusion | flops 553648128 | bytes 1572864 | tf_op jit(solution)/shard_map/snj,nk->sjk/dot_general | solution.py:40
  122.5 16.0 %fusion.50 = f32[1024,2,128]{2,0,1:T(8,128)S(1)} fusion(bf16[2,4,1024,128]{3,2,0,1:T(8,128)(2,1)S(1)} %bitcast.192), kind=kOutput, calls=%fused_computation.48 | convolution fusion | flops 553648128 | bytes 1572864 | tf_op jit(solution)/shard_map/snj,nk->sjk/dot_general | solution.py:40
  138.5 15.8 %fusion.69 = f32[2,128,1024]{1,2,0:T(8,128)S(1)} fusion(f32[1024,2,128]{2,0,1:T(8,128)S(1)} %fusion.48, bf16[2,4,1024,128]{3,2,0,1:T(8,128)(2,1)S(1)} %bitcast.193), kind=kOutput, calls=%fused_computation.56 | convolution fusion | flops 552861696 | bytes 2621440 | tf_op jit(solution)/shard_map/snj,nk->sjk/dot_general | solution.py:43
  154.4 16.2 %fusion.75 = f32[2,128,1024]{1,2,0:T(8,128)S(1)} fusion(f32[1024,2,128]{2,0,1:T(8,128)S(1)} %fusion.46, bf16[2,4,1024,128]{3,2,0,1:T(8,128)(2,1)S(1)} %bitcast.194), kind=kOutput, calls=%fused_computation.58 | convolution fusion | flops 552861696 | bytes 2621440 | tf_op jit(solution)/shard_map/snj,nk->sjk/dot_general | solution.py:38
  170.6 15.8 %fusion.63 = f32[2,128,1024]{1,2,0:T(8,128)S(1)} fusion(f32[1024,2,128]{2,0,1:T(8,128)S(1)} %fusion.50, bf16[2,4,1024,128]{3,2,0,1:T(8,128)(2,1)S(1)} %bitcast.195), kind=kOutput, calls=%fused_computation.54 | convolution fusion | flops 552861696 | bytes 2621440 | tf_op jit(solution)/shard_map/snj,nk->sjk/dot_general | solution.py:38
  186.4 18.2 %fusion.89 = (bf16[2,1,128,1024]{2,3,0,1:T(8,128)(2,1)S(1)}, bf16[2,1,128,1024]{2,3,0,1:T(8,128)(2,1)S(1)}, bf16[2,1,128,1024]{2,3,0,1:T(8,128)(2,1)S(1)}, bf16[2,1,128,1024]{2,3,0,1:T(8,128)(2,1)S(1)}) fusion(f32[2,128,1024]{1,2,0:T(8,128)S(1)} %fusion.69, f32[2,128,1024]{1,2,0:T(8,128)S(1)} %fusion.63, f32[128,1024]{0,1:T(8,128)S(1)} %get-tuple-element.54, ...), kind=kOutput, calls=%fused_computation.75 | convolution fusion | flops 557056000 | bytes 7864320 | tf_op jit(solution)/shard_map/snj,nk->sjk/dot_general | solution.py:43
  204.9 3.5 copy.8
  208.4 11.2 %all-to-all-start.1 = ((bf16[2,4,128,1024]{2,0,1,3:T(2,128)(2,1)}), bf16[2,4,128,1024]{2,0,1,3:T(2,128)(2,1)S(1)}, u32[]{:S(2)}, u32[]{:S(2)}) async-start(bf16[2,4,128,1024]{2,0,1,3:T(2,128)(2,1)} %copy.8), calls=%async_computation.1 | async-start | bytes 4194304 | tf_op jit(solution)/shard_map/all_to_all | solution.py:91
  219.8 40.7 %all-to-all-done.1 = bf16[2,4,128,1024]{2,0,1,3:T(2,128)(2,1)S(1)} async-done(((bf16[2,4,128,1024]{2,0,1,3:T(2,128)(2,1)}), bf16[2,4,128,1024]{2,0,1,3:T(2,128)(2,1)S(1)}, u32[]{:S(2)}, u32[]{:S(2)}) %all-to-all-start.1) | async-done | bytes 2097184 | tf_op jit(solution)/shard_map/all_to_all | solution.py:91
  260.6 2.7 copy.11
  263.2 2.8 all_to_all.33
  266.1 62.7 %fusion.8 = f32[2,64,2048]{2,1,0:T(8,128)S(1)} fusion(bf16[2,4,2048,64]{2,3,0,1:T(8,128)(2,1)S(1)} %all_to_all.33), kind=kOutput, calls=%fused_computation.17 | convolution fusion | flops 1140850688 | bytes 1572864 | tf_op jit(solution)/shard_map/sjk,jm->skm/dot_general | solution.py:41
  328.8 63.0 %fusion.12 = f32[2,64,2048]{2,1,0:T(8,128)S(1)} fusion(bf16[2,4,2048,64]{2,3,0,1:T(8,128)(2,1)S(1)} %all_to_all.33), kind=kOutput, calls=%fused_computation.19 | convolution fusion | flops 1140850688 | bytes 1572864 | tf_op jit(solution)/shard_map/sjk,jm->skm/dot_general | solution.py:41
  391.8 62.7 %fusion.10 = f32[2,64,2048]{2,1,0:T(8,128)S(1)} fusion(bf16[2,4,2048,64]{2,3,0,1:T(8,128)(2,1)S(1)} %all_to_all.33), kind=kOutput, calls=%fused_computation.18 | convolution fusion | flops 1140850688 | bytes 1572864 | tf_op jit(solution)/shard_map/sjk,jm->skm/dot_general | solution.py:40
  454.5 63.1 %fusion.14 = f32[2,64,2048]{2,1,0:T(8,128)S(1)} fusion(bf16[2,4,2048,64]{2,3,0,1:T(8,128)(2,1)S(1)} %all_to_all.33), kind=kOutput, calls=%fused_computation.20 | convolution fusion | flops 1140850688 | bytes 1572864 | tf_op jit(solution)/shard_map/sjk,jm->skm/dot_general | solution.py:40
  517.7 61.5 %fusion.33 = f32[2,64,2048]{2,1,0:T(8,128)S(1)} fusion(f32[2,64,2048]{2,1,0:T(8,128)S(1)} %fusion.12, bf16[2,4,2048,64]{2,3,0,1:T(8,128)(2,1)S(1)} %all_to_all.33), kind=kOutput, calls=%fused_computation.38 | convolution fusion | flops 1136918528 | bytes 2621440 | tf_op jit(solution)/shard_map/sjk,jm->skm/dot_general | solution.py:43
  579.2 61.9 %fusion.36 = f32[2,64,2048]{2,1,0:T(8,128)S(1)} fusion(f32[2,64,2048]{2,1,0:T(8,128)S(1)} %fusion.10, bf16[2,4,2048,64]{2,3,0,1:T(8,128)(2,1)S(1)} %all_to_all.33), kind=kOutput, calls=%fused_computation.39 | convolution fusion | flops 1136918528 | bytes 2621440 | tf_op jit(solution)/shard_map/sjk,jm->skm/dot_general | solution.py:38
  641.1 61.7 %fusion.30 = f32[2,64,2048]{2,1,0:T(8,128)S(1)} fusion(f32[2,64,2048]{2,1,0:T(8,128)S(1)} %fusion.14, bf16[2,4,2048,64]{2,3,0,1:T(8,128)(2,1)S(1)} %all_to_all.33), kind=kOutput, calls=%fused_computation.37 | convolution fusion | flops 1136918528 | bytes 2621440 | tf_op jit(solution)/shard_map/sjk,jm->skm/dot_general | solution.py:38
  702.9 61.9 %subtract_divide_fusion = f32[2,64,2048]{2,1,0:T(8,128)S(1)} fusion(f32[2,64,2048]{2,1,0:T(8,128)S(1)} %fusion.33, f32[2,64,2048]{2,1,0:T(8,128)S(1)} %fusion.30, f32[2,64,2048]{2,1,0:T(8,128)S(1)} %fusion.36, f32[2,64,2048]{2,1,0:T(8,128)S(1)} %fusion.8, f32[2]{0:T(128)S(1)} %subtract_multiply_fusion, f32[2]{0:T(128)S(1)} %get-tuple-element.21, ...), kind=kOutput, calls=%fused_computation.62 | convolution fusion | flops 1140850688 | bytes 5769216 | tf_op jit(solution)/shard_map/sjk,jm->skm/dot_general | solution.py:43
  765.8 8.9 %collective-permute-start.1 = (f32[2,8,2048]{2,1,0:T(8,128)S(1)}, f32[2,8,2048]{2,1,0:T(8,128)S(1)}, u32[]{:S(2)}, u32[]{:S(2)}) collective-permute-start(f32[2,8,2048]{2,1,0:T(8,128)S(1)} %get-tuple-element.48), channel_id=1, source_target_pairs={{1,0},{2,1},{3,2},{4,3},{5,4},{6,5},{7,6},{8,7},{9,8},{10,9},{11,1... | collective-permute-start | bytes 393224 | tf_op jit(solution)/shard_map/ppermute | solution.py:23
  777.9 2.5 broadcast.127.clone
  780.4 16.5 %while.2 = (s32[]{:T(128)}, f32[80,2048]{1,0:T(8,128)S(1)}, s32[8,2]{0,1:T(2,128)S(1)}, f32[8,64,2048]{2,1,0:T(8,128)}, s32[]{:T(128)}) while((s32[]{:T(128)}, f32[80,2048]{1,0:T(8,128)S(1)}, s32[8,2]{0,1:T(2,128)S(1)}, f32[8,64,2048]{2,1,0:T(8,128)}, s32[]{:T(128)}) %tuple.38), condition=%wide.while_cond, body=%wide.while_body.sunk | while | flops 2 | bytes 1049189 | solution.py:107
  799.3 16.6 %while.3 = (s32[]{:T(128)}, f32[80,2048]{1,0:T(8,128)S(1)}, s32[8,2]{0,1:T(2,128)S(1)}, f32[8,64,2048]{2,1,0:T(8,128)}, s32[]{:T(128)}) while((s32[]{:T(128)}, f32[80,2048]{1,0:T(8,128)S(1)}, s32[8,2]{0,1:T(2,128)S(1)}, f32[8,64,2048]{2,1,0:T(8,128)}, s32[]{:T(128)}) %tuple.41), condition=%wide.while_cond.1, body=%wide.while_body.1.sunk | while | flops 2 | bytes 1049189 | solution.py:107
  815.9 6.7 add_multiply_fusion
  (72 shorter events, 42.2 us)
Async XLA Ops:
  14.5 48.4 %all-to-all-start = ((bf16[16,2,32768]{2,1,0:T(2,128)(2,1)}), bf16[16,2,32768]{2,1,0:T(2,128)(2,1)S(1)}, u32[]{:S(2)}, u32[]{:S(2)}) async-start(bf16[16,2,32768]{2,1,0:T(2,128)(2,1)} %reshape.137), calls=%async_computation | async-start | bytes 4194304 | tf_op jit(solution)/shard_map/all_to_all | solution.py:82
  204.9 14.7 %copy-start = (f32[2,3]{1,0:T(2,128)S(1)}, f32[2,3]{1,0:T(2,128)}, u32[]{:S(2)}) copy-start(f32[2,3]{1,0:T(2,128)} %param.4) | copy-start | bytes 76
  208.4 52.2 %all-to-all-start.1 = ((bf16[2,4,128,1024]{2,0,1,3:T(2,128)(2,1)}), bf16[2,4,128,1024]{2,0,1,3:T(2,128)(2,1)S(1)}, u32[]{:S(2)}, u32[]{:S(2)}) async-start(bf16[2,4,128,1024]{2,0,1,3:T(2,128)(2,1)} %copy.8), calls=%async_computation.1 | async-start | bytes 4194304 | tf_op jit(solution)/shard_map/all_to_all | solution.py:91
  702.8 71.9 %copy-start.1 = (s32[8,2]{0,1:T(2,128)S(1)}, s32[8,2]{0,1:T(2,128)}, u32[]{:S(2)}) copy-start(s32[8,2]{0,1:T(2,128)} %param.5) | copy-start | bytes 196
  764.8 12.6 %collective-permute-start = (f32[2,8,2048]{2,1,0:T(8,128)S(1)}, f32[2,8,2048]{2,1,0:T(8,128)S(1)}, u32[]{:S(2)}, u32[]{:S(2)}) collective-permute-start(f32[2,8,2048]{2,1,0:T(8,128)S(1)} %get-tuple-element.47), channel_id=1, source_target_pairs={{0,1},{1,2},{2,3},{3,4},{4,5},{5,6},{6,7},{7,8},{8,9},{9,10},{10,1... | collective-permute-start | bytes 393224 | tf_op jit(solution)/shard_map/ppermute | solution.py:21
  765.8 11.5 %collective-permute-start.1 = (f32[2,8,2048]{2,1,0:T(8,128)S(1)}, f32[2,8,2048]{2,1,0:T(8,128)S(1)}, u32[]{:S(2)}, u32[]{:S(2)}) collective-permute-start(f32[2,8,2048]{2,1,0:T(8,128)S(1)} %get-tuple-element.48), channel_id=1, source_target_pairs={{1,0},{2,1},{3,2},{4,3},{5,4},{6,5},{7,6},{8,7},{9,8},{10,9},{11,1... | collective-permute-start | bytes 393224 | tf_op jit(solution)/shard_map/ppermute | solution.py:23
where the time goes:
time: 827 us; the launch traced here: 823 us
  matrix products  629 us (76%)
  waiting for transfers between devices  82.1 us (10%)
  local copies, waits for them, and re-layouts  72.7 us (9%)
  starting transfers between devices  28.6 us (3%)
  other arithmetic  9.56 us (1%)
    dot_general x4, matrix products, complex_dft(): jnp.einsum(formula, x_imag, w_imag, preferred_element_type=jnp.float32)  158 us
    dot_general x4, matrix products, complex_dft(): jnp.einsum(formula, x_real, w_imag, preferred_element_type=jnp.float32)  158 us
    dot_general x4, matrix products, complex_dft(): jnp.einsum(formula, x_imag, w_real, preferred_element_type=jnp.float32)  157 us
    dot_general x4, matrix products, complex_dft(): jnp.einsum(formula, x_real, w_real, preferred_element_type=jnp.float32)  156 us
    all_to_all x1, waiting for transfers between devices, local(): lax.all_to_all(twiddled, 'tm', split_axis=3, concat_axis=2, tiled=True)  40.7 us
    all_to_all x1, waiting for transfers between devices, local(): lax.all_to_all(series, 'tm', split_axis=3, concat_axis=2, tiled=True)  38.9 us
    gather x48, local copies, waits for them, and re-layouts  33 us
    unnamed x9, local copies, waits for them, and re-layouts  24.4 us
  transfers between devices with their start and end apart: 4, of which 3 were waited for; matrix products, arithmetic and copies ran while one was open for 0% of the time, Pallas kernels for 0%

commit v1 on v0

v1 whole, which is shorter than its diff:
```python
import functools
import math

import jax
import jax.numpy as jnp
from jax import lax
from jax.experimental import pallas as pl
from jax.experimental.pallas import tpu as pltpu
from jax.sharding import PartitionSpec as P

DMAX = 8
LOW = 64


def unit(products, length):
    angle = products.astype(jnp.float32) * (2.0 * math.pi / length)
    return jnp.cos(angle), -jnp.sin(angle)


def dft_table(length):
    bins = jnp.arange(length, dtype=jnp.int32)[None, :]
    high = LOW * jnp.arange(length // LOW, dtype=jnp.int32)[:, None]
    low = jnp.arange(LOW, dtype=jnp.int32)[:, None]
    thin = unit(high * bins % length, length) + unit(low * bins % length, length)
    high_real, high_imag, low_real, low_imag = lax.optimization_barrier(thin)
    high_real, high_imag = high_real[:, None], high_imag[:, None]
    real = (high_real * low_real - high_imag * low_imag).astype(jnp.bfloat16)
    imag = (high_real * low_imag + high_imag * low_real).astype(jnp.bfloat16)
    return real.reshape(length, length), imag.reshape(length, length)


def dot(x, y):
    return jnp.dot(x, y, preferred_element_type=jnp.float32)


def first_kernel(x_ref, wr_ref, wi_ref, tr_ref, ti_ref, out_ref):
    width = x_ref.shape[-1]
    if width % 128 == 0:
        both = jnp.concatenate([x_ref[0, 0], x_ref[0, 1]], axis=-1)
        by_real = dot(wr_ref[...], both)
        by_imag = dot(wi_ref[...], both)
        real = by_real[:, :width] - by_imag[:, width:]
        imag = by_imag[:, :width] + by_real[:, width:]
    else:
        real = dot(wr_ref[...], x_ref[0, 0]) - dot(wi_ref[...], x_ref[0, 1])
        imag = dot(wi_ref[...], x_ref[0, 0]) + dot(wr_ref[...], x_ref[0, 1])
    tr, ti = tr_ref[...], ti_ref[...]
    out_ref[0, 0] = (real * tr - imag * ti).astype(jnp.bfloat16)
    out_ref[0, 1] = (real * ti + imag * tr).astype(jnp.bfloat16)


def first_stage(members, table, twiddle):
    segs, comps, rows, width = members.shape
    tile = min(256, rows)
    whole = pl.BlockSpec((1, 2, rows, width), lambda s, c, r: (s, c, 0, 0))
    strip = pl.BlockSpec((tile, rows), lambda s, c, r: (r, 0))
    turn = pl.BlockSpec((tile, width), lambda s, c, r: (r, 0))
    return pl.pallas_call(
        first_kernel,
        grid=(segs, comps // 2, rows // tile),
        in_specs=[whole, strip, strip, turn, turn],
        out_specs=pl.BlockSpec((1, 2, tile, width), lambda s, c, r: (s, c, r, 0)),
        out_shape=jax.ShapeDtypeStruct(members.shape, jnp.bfloat16),
    )(members, *table, *twiddle)


def second_kernel(bins, coef_ref, x_ref, wr_ref, wi_ref, out_ref):
    segs, comps, rows, length = x_ref.shape
    flat = x_ref[...].reshape(segs * comps * rows, length)
    by_real = dot(flat, wr_ref[...]).reshape(segs, comps, rows, -1)
    by_imag = dot(flat, wi_ref[...]).reshape(segs, comps, rows, -1)
    for s in range(segs):
        ar = by_real[s, 0] - by_imag[s, 1]
        ai = by_imag[s, 0] + by_real[s, 1]
        br = by_real[s, 2] - by_imag[s, 3]
        bi = by_imag[s, 2] + by_real[s, 3]
        a, b, c = coef_ref[s, 0], coef_ref[s, 1], coef_ref[s, 2]
        numer = b * (ar * ar + ai * ai) + a * (br * br + bi * bi) - 2.0 * c * (ar * br + ai * bi)
        out_ref[s] = numer / ((a * b - c * c) * bins)


def second_stage(members, table, antenna, bins):
    segs, comps, rows, length = members.shape
    tile = min(512, length)
    column = pl.BlockSpec((length, tile), lambda k: (0, k))
    return pl.pallas_call(
        functools.partial(second_kernel, float(bins)),
        grid=(length // tile,),
        in_specs=[
            pl.BlockSpec(memory_space=pltpu.SMEM),
            pl.BlockSpec(members.shape, lambda k: (0, 0, 0, 0)),
            column,
            column,
        ],
        out_specs=pl.BlockSpec((segs, rows, tile), lambda k: (0, 0, k)),
        out_shape=jax.ShapeDtypeStruct((segs, rows, length), jnp.float32),
    )(antenna, members, *table)


def shifted(wide, s, start, rows):
    part = lax.rem(start, 8)
    base = pl.multiple_of(start - part, 8)
    tiles = wide[s, pl.ds(base, rows + 8), :].reshape(rows // 8 + 1, 8, -1)
    turned = pltpu.roll(tiles, lax.rem(8 - part, 8), 1)
    here = lax.broadcasted_iota(jnp.int32, turned[1:].shape, 1) < 8 - part
    return jnp.where(here, turned[:-1], turned[1:]).reshape(rows, -1)


def detect_kernel(last, place_ref, off_ref, low_ref, mid_ref, up_ref, out_ref, wide):
    segs, rows, length = mid_ref.shape
    t = pl.program_id(0)

    @pl.when(t == 0)
    def _():
        wide[:, DMAX : DMAX + rows] = mid_ref[...]
        for s in range(segs):
            low, up = low_ref[s], up_ref[s]
            wide[s, :DMAX] = jnp.where(place_ref[0] == 0, pltpu.roll(low, 1, 1), low)
            wide[s, DMAX + rows : 2 * DMAX + rows] = jnp.where(
                place_ref[0] == last, pltpu.roll(up, length - 1, 1), up
            )

    total = shifted(wide, 0, DMAX + off_ref[t, 0], rows)
    for s in range(1, segs):
        total = total + shifted(wide, s, DMAX + off_ref[t, s], rows)
    out_ref[0] = total / segs


def detect(fstat, offsets):
    segs, rows, length = fstat.shape
    count = lax.axis_size("tm")
    lower = lax.ppermute(
        fstat[:, rows - DMAX :], "tm", [(i, (i + 1) % count) for i in range(count)]
    )
    upper = lax.ppermute(fstat[:, :DMAX], "tm", [((i + 1) % count, i) for i in range(count)])
    place = lax.axis_index("tm").reshape(1)
    templates = offsets.shape[0]
    smem = pl.BlockSpec(memory_space=pltpu.SMEM)
    rim = pl.BlockSpec((segs, DMAX, length), lambda t: (0, 0, 0))
    return pl.pallas_call(
        functools.partial(detect_kernel, count - 1),
        grid=(templates,),
        in_specs=[smem, smem, rim, pl.BlockSpec(fstat.shape, lambda t: (0, 0, 0)), rim],
        out_specs=pl.BlockSpec((1, rows, length), lambda t: (t, 0, 0)),
        out_shape=jax.ShapeDtypeStruct((templates, rows, length), jnp.float32),
        scratch_shapes=[pltpu.VMEM((segs, rows + 3 * DMAX, length), jnp.float32)],
    )(place, offsets, lower, fstat, upper)


def local(series, antenna, offsets):
    count = lax.axis_size("tm")
    rows, length = series.shape[2] * count, series.shape[3]
    width = length // count
    bins = rows * length
    columns = lax.axis_index("tm") * width + jnp.arange(width, dtype=jnp.int32)
    turns = jnp.arange(rows, dtype=jnp.int32)[:, None] * columns[None, :] % bins
    twiddle = unit(turns, bins)
    short, long = dft_table(rows), dft_table(length)
    members = lax.all_to_all(series, "tm", split_axis=3, concat_axis=2, tiled=True)
    twiddled = first_stage(members, short, twiddle)
    members = lax.all_to_all(twiddled, "tm", split_axis=2, concat_axis=3, tiled=True)
    fstat = second_stage(members, long, antenna, bins)
    return detect(fstat, offsets)


def solution(mesh):
    return jax.shard_map(
        local,
        mesh=mesh,
        in_specs=(P("sky", None, "tm", None), P("sky", None), P("sky", None)),
        out_specs=P("sky", "tm", None),
        check_vma=False,
    )
```

time: 827 us -> 189 us (0.23)
  matrix products: 629 us -> 0 us
  Pallas kernels: 0 us -> 34.8 us
  local copies, waits for them, and re-layouts: 72.7 us -> 40.2 us
  waiting for transfers between devices: 82.1 us -> 64.8 us
  other arithmetic: 9.56 us -> 19.1 us
    dot_general x16 -> x0, matrix products: 629 us -> none  [the longest x4 158 us: complex_dft(): jnp.einsum(formula, x_imag, w_imag, preferred_element_type=jnp.float32)]
    pallas_call x0 -> x3, Pallas kernels: none -> 34.8 us  [the longest x1 16.3 us: first_stage(): pl.pallas_call(first_kernel, grid=(segs, comps // 2, rows // tile), in_sp...]
    gather x48 -> x0, local copies, waits for them, and re-layouts: 33 us -> none
    convert_element_type x0 -> x2, other arithmetic: none -> 11.5 us  [dft_table(): imag = (high_real * low_imag + high_imag * low_real).astype(jnp.bfloat16)]
    all_to_all x1, waiting for transfers between devices: 40.7 us -> 29.5 us  [local(): lax.all_to_all(twiddled, 'tm', split_axis=2, concat_axis=3, tiled=True)]
    unnamed x9 -> x10, local copies, waits for them, and re-layouts: 24.4 us -> 20.8 us
  transfers between devices with their start and end apart: 4 -> 4, of which waited for: 3 -> 3; matrix products, arithmetic and copies ran while one was open for 0% -> 11% of each run, Pallas kernels for 0% -> 0%
where the time goes in v1:
time: 189 us; the launch traced here: 187 us
  waiting for transfers between devices  64.8 us (34%)
  local copies, waits for them, and re-layouts  40.2 us (21%)
  Pallas kernels  34.8 us (18%)
  starting transfers between devices  28.6 us (15%)
  other arithmetic  19.1 us (10%)
    all_to_all x1, waiting for transfers between devices, local(): lax.all_to_all(series, 'tm', split_axis=3, concat_axis=2, tiled=True)  33.3 us
    all_to_all x1, waiting for transfers between devices, local(): lax.all_to_all(twiddled, 'tm', split_axis=2, concat_axis=3, tiled=True)  29.5 us
    unnamed x10, local copies, waits for them, and re-layouts  20.8 us
    pallas_call x1, Pallas kernels, first_stage(): pl.pallas_call(first_kernel, grid=(segs, comps // 2, rows // tile), in_sp...  16.3 us
    pallas_call x1, Pallas kernels, second_stage(): pl.pallas_call(functools.partial(second_kernel, float(bins)), grid=(lengt...  13.2 us
    convert_element_type x2, other arithmetic, dft_table(): imag = (high_real * low_imag + high_imag * low_real).astype(jnp.bfloat16)  11.5 us
    all_to_all x1, starting transfers between devices, local(): lax.all_to_all(twiddled, 'tm', split_axis=2, concat_axis=3, tiled=True)  11.2 us
    ppermute x1, starting transfers between devices, detect(): lax.ppermute(fstat[:, :DMAX], 'tm', [((i + 1) % count, i) for i in range(...  8.93 us
  transfers between devices with their start and end apart: 4, of which 3 were waited for; matrix products, arithmetic and copies ran while one was open for 11% of the time, Pallas kernels for 0%

profile of v1, /device:TPU:0, one launch (start us, length us, event | category | flops | bytes accessed | tf_op | source)
XLA Modules:
  0.0 187.4 jit_solution(11530790634426500799)
XLA Ops:
  0.0 7.0 %copy.7 = bf16[2,4,64,2048]{2,1,0,3:T(4,128)(2,1)} copy(bf16[2,4,64,2048]{3,2,1,0:T(8,128)(2,1)} %param.3) | data formatting | bytes 4194304 | tf_op args[0]
  7.0 7.5 %reshape.62 = bf16[16,2,32768]{2,1,0:T(2,128)(2,1)} reshape(bf16[2048,2,4,64]{3,2,1,0:T(4,128)(2,1)} %bitcast.20) | data formatting | bytes 4194304
  14.5 7.4 %all-to-all-start = ((bf16[16,2,32768]{2,1,0:T(2,128)(2,1)}), bf16[16,2,32768]{2,1,0:T(2,128)(2,1)S(1)}, u32[]{:S(2)}, u32[]{:S(2)}) async-start(bf16[16,2,32768]{2,1,0:T(2,128)(2,1)} %reshape.62), calls=%async_computation | async-start | bytes 4194304 | tf_op jit(solution)/shard_map/all_to_all | solution.py:159
  22.0 1.0 sine_negate_fusion.3
  23.0 0.3 sine_negate_fusion.4
  23.4 3.0 %sine_negate_fusion.1 = (f32[1024,128]{1,0:T(8,128)}, f32[1024,128]{1,0:T(8,128)}) fusion(s32[128]{0:T(128)S(1)} %iota_add_fusion), kind=kLoop, calls=%fused_computation.20 | loop fusion | flops 1966080 | bytes 1049088 | tf_op jit(solution)/shard_map/neg | solution.py:17
  26.3 3.3 %add_convert_fusion.1 = (bf16[16,64,1024]{2,1,0:T(8,128)(2,1)}, bf16[16,64,1024]{2,1,0:T(8,128)(2,1)}) fusion(f32[64,1024]{1,0:T(8,128)S(1)} %get-tuple-element.16, f32[16,1024]{1,0:T(8,128)S(1)} %get-tuple-element.15, f32[64,1024]{1,0:T(8,128)S(1)} %get-tuple-element.14, f32[16,1024]{1,0:T(8,128)S(1)} %get-tuple-element.13), kind=kLoop, calls=%fused_computation.2 | loop fusion | flops 8388608 | bytes 4849664 | tf_op jit(solution)/shard_map/convert_element_type | solution.py:28
  29.6 33.3 %all-to-all-done = bf16[16,2,32768]{2,1,0:T(2,128)(2,1)S(1)} async-done(((bf16[16,2,32768]{2,1,0:T(2,128)(2,1)}), bf16[16,2,32768]{2,1,0:T(2,128)(2,1)S(1)}, u32[]{:S(2)}, u32[]{:S(2)}) %all-to-all-start) | async-done | bytes 2097184 | tf_op jit(solution)/shard_map/all_to_all | solution.py:159
  62.9 4.9 %reshape.63 = bf16[2048,2,4,64]{3,2,1,0:T(4,128)(2,1)} reshape(bf16[16,2,32768]{2,1,0:T(2,128)(2,1)S(1)} %all-to-all-done) | data formatting | bytes 4194304
  67.9 7.0 %copy.8 = bf16[2,4,64,16,128]{4,2,3,1,0:T(8,128)(2,1)} copy(bf16[2,4,64,16,128]{2,1,0,4,3:T(4,128)(2,1)} %bitcast.19) | data formatting | bytes 4194304 | tf_op jit(solution)/shard_map/all_to_all | solution.py:159
  74.8 16.3 %shard_map.37 = bf16[2,4,1024,128]{3,2,1,0:T(8,128)(2,1)} custom-call(bf16[2,4,1024,128]{3,2,1,0:T(8,128)(2,1)} %bitcast.24, bf16[1024,1024]{1,0:T(8,128)(2,1)} %bitcast.23, bf16[1024,1024]{1,0:T(8,128)(2,1)} %bitcast.22, f32[1024,128]{1,0:T(8,128)} %get-tuple-element.30.tr_ref, f32[1024,128]{1,0:T(8,128)} %get-tuple-element.29.ti_ref), custom_call_target="tpu_custom_call" | custom-call | tf_op jit(solution)/shard_map/pallas_call | solution.py:58
  91.1 4.5 %copy.9 = bf16[2,4,1024,128]{3,1,0,2:T(4,128)(2,1)} copy(bf16[2,4,1024,128]{3,2,1,0:T(8,128)(2,1)} %shard_map.37) | data formatting | bytes 4194304 | tf_op jit(solution)/shard_map/pallas_call | solution.py:58
  95.6 11.2 %all-to-all-start.1 = ((bf16[2,4,1024,128]{3,1,0,2:T(4,128)(2,1)}), bf16[2,4,1024,128]{3,1,0,2:T(4,128)(2,1)S(1)}, u32[]{:S(2)}, u32[]{:S(2)}) async-start(bf16[2,4,1024,128]{3,1,0,2:T(4,128)(2,1)} %copy.9), calls=%async_computation.1 | async-start | bytes 4194304 | tf_op jit(solution)/shard_map/all_to_all | solution.py:161
  106.9 2.1 %sine_negate_fusion = (f32[64,2048]{1,0:T(8,128)S(1)}, f32[64,2048]{1,0:T(8,128)S(1)}) fusion(), kind=kLoop, calls=%fused_computation.17 | loop fusion | flops 1966080 | bytes 1048576 | tf_op jit(solution)/shard_map/neg | solution.py:17
  108.9 1.1 sine_negate_fusion.2
  110.1 8.2 %add_convert_fusion = (bf16[32,64,2048]{2,1,0:T(8,128)(2,1)}, bf16[32,64,2048]{2,1,0:T(8,128)(2,1)}) fusion(f32[64,2048]{1,0:T(8,128)S(1)} %get-tuple-element.20, f32[32,2048]{1,0:T(8,128)S(1)} %get-tuple-element.19, f32[64,2048]{1,0:T(8,128)S(1)} %get-tuple-element.18, f32[32,2048]{1,0:T(8,128)S(1)} %get-tuple-element.17), kind=kLoop, calls=%fused_computation | loop fusion | flops 33554432 | bytes 18350080 | tf_op jit(solution)/shard_map/convert_element_type | solution.py:28
  118.3 29.5 %all-to-all-done.1 = bf16[2,4,1024,128]{3,1,0,2:T(4,128)(2,1)S(1)} async-done(((bf16[2,4,1024,128]{3,1,0,2:T(4,128)(2,1)}), bf16[2,4,1024,128]{3,1,0,2:T(4,128)(2,1)S(1)}, u32[]{:S(2)}, u32[]{:S(2)}) %all-to-all-start.1) | async-done | bytes 2097184 | tf_op jit(solution)/shard_map/all_to_all | solution.py:161
  147.8 2.7 %copy.13 = bf16[2,4,16,64,128]{4,2,3,1,0:T(8,128)(2,1)} copy(bf16[2,4,16,64,128]{4,1,0,3,2:T(4,128)(2,1)S(1)} %bitcast.21) | data formatting | bytes 4194304 | tf_op jit(solution)/shard_map/all_to_all | solution.py:161
  150.5 4.2 %all_to_all.33.x_ref = bf16[2,4,64,2048]{3,2,1,0:T(8,128)(2,1)} reshape(bf16[2,4,64,16,128]{4,3,2,1,0:T(8,128)(2,1)} %bitcast.25) | data formatting | bytes 4194304 | tf_op jit(solution)/shard_map/all_to_all | solution.py:161
  154.7 0.0 copy-start.2
  154.7 13.2 %shard_map.38.mid_ref = f32[2,64,2048]{2,1,0:T(8,128)} custom-call(f32[2,3]{1,0:T(2,128)} %coef_ref.1, bf16[2,4,64,2048]{3,2,1,0:T(8,128)(2,1)} %all_to_all.33.x_ref, bf16[2048,2048]{1,0:T(8,128)(2,1)} %bitcast.18, bf16[2048,2048]{1,0:T(8,128)(2,1)} %bitcast.17), custom_call_target="tpu_custom_call" | custom-call | tf_op jit(solution)/shard_map/pallas_call | solution.py:86
  167.9 1.0 fusion.35
  168.9 1.0 collective-permute-start
  169.9 8.9 %collective-permute-start.1 = (f32[2,8,2048]{2,1,0:T(8,128)S(1)}, f32[2,8,2048]{2,1,0:T(8,128)S(1)}, u32[]{:S(2)}, u32[]{:S(2)}) collective-permute-start(f32[2,8,2048]{2,1,0:T(8,128)S(1)} %get-tuple-element.23), channel_id=1, source_target_pairs={{1,0},{2,1},{3,2},{4,3},{5,4},{6,5},{7,6},{8,7},{9,8},{10,9},{11,1... | collective-permute-start | bytes 393224 | tf_op jit(solution)/shard_map/ppermute | solution.py:135
  178.9 0.0 copy-done.2
  178.9 0.7 copy.11.off_ref
  179.5 1.9 %collective-permute-done.low_ref = f32[2,8,2048]{2,1,0:T(8,128)S(1)} collective-permute-done((f32[2,8,2048]{2,1,0:T(8,128)S(1)}, f32[2,8,2048]{2,1,0:T(8,128)S(1)}, u32[]{:S(2)}, u32[]{:S(2)}) %collective-permute-start) | collective-permute-done | bytes 131104 | tf_op jit(solution)/shard_map/ppermute | solution.py:132
  181.5 0.0 copy-start
  181.5 0.0 collective-permute-done.1.up_ref
  181.5 0.6 copy-done
  182.1 0.0 copy-done.1
  182.2 5.2 %shard_map.39 = f32[8,64,2048]{2,1,0:T(8,128)} custom-call(s32[1]{0:T(128)} %bitcast.place_ref, s32[8,2]{1,0:T(8,128)} %copy.11.off_ref, f32[2,8,2048]{2,1,0:T(8,128)} %copy-done, f32[2,64,2048]{2,1,0:T(8,128)} %shard_map.38.mid_ref, f32[2,8,2048]{2,1,0:T(8,128)} %copy-done.1), custom_call_target="tpu_custom_call" | custom-call | tf_op jit(solution)/shard_map/pallas_call | solution.py:140
  (4 shorter events, 0.0 us)
Async XLA Ops:
  14.5 48.4 %all-to-all-start = ((bf16[16,2,32768]{2,1,0:T(2,128)(2,1)}), bf16[16,2,32768]{2,1,0:T(2,128)(2,1)S(1)}, u32[]{:S(2)}, u32[]{:S(2)}) async-start(bf16[16,2,32768]{2,1,0:T(2,128)(2,1)} %reshape.62), calls=%async_computation | async-start | bytes 4194304 | tf_op jit(solution)/shard_map/all_to_all | solution.py:159
  95.6 52.2 %all-to-all-start.1 = ((bf16[2,4,1024,128]{3,1,0,2:T(4,128)(2,1)}), bf16[2,4,1024,128]{3,1,0,2:T(4,128)(2,1)S(1)}, u32[]{:S(2)}, u32[]{:S(2)}) async-start(bf16[2,4,1024,128]{3,1,0,2:T(4,128)(2,1)} %copy.9), calls=%async_computation.1 | async-start | bytes 4194304 | tf_op jit(solution)/shard_map/all_to_all | solution.py:161
  154.7 24.2 %copy-start.2 = (s32[8,2]{0,1:T(2,128)S(1)}, s32[8,2]{0,1:T(2,128)}, u32[]{:S(2)}) copy-start(s32[8,2]{0,1:T(2,128)} %param.5) | copy-start | bytes 196
  168.9 12.5 %collective-permute-start = (f32[2,8,2048]{2,1,0:T(8,128)S(1)}, f32[2,8,2048]{2,1,0:T(8,128)S(1)}, u32[]{:S(2)}, u32[]{:S(2)}) collective-permute-start(f32[2,8,2048]{2,1,0:T(8,128)S(1)} %get-tuple-element.24), channel_id=1, source_target_pairs={{0,1},{1,2},{2,3},{3,4},{4,5},{5,6},{6,7},{7,8},{8,9},{9,10},{10,1... | collective-permute-start | bytes 393224 | tf_op jit(solution)/shard_map/ppermute | solution.py:132
  169.9 11.5 %collective-permute-start.1 = (f32[2,8,2048]{2,1,0:T(8,128)S(1)}, f32[2,8,2048]{2,1,0:T(8,128)S(1)}, u32[]{:S(2)}, u32[]{:S(2)}) collective-permute-start(f32[2,8,2048]{2,1,0:T(8,128)S(1)} %get-tuple-element.23), channel_id=1, source_target_pairs={{1,0},{2,1},{3,2},{4,3},{5,4},{6,5},{7,6},{8,7},{9,8},{10,9},{11,1... | collective-permute-start | bytes 393224 | tf_op jit(solution)/shard_map/ppermute | solution.py:135
  181.5 0.7 copy-start
  181.5 0.7 copy-start.1

commit v2 on v1

--- a/solution.py
+++ b/solution.py
@@ -17,15 +17,24 @@
     return jnp.cos(angle), -jnp.sin(angle)
 
 
+def thin_tables(length, columns, rows, low_rows):
+    columns = columns[None, :]
+    high = low_rows * jnp.arange(rows // low_rows, dtype=jnp.int32)[:, None]
+    low = jnp.arange(low_rows, dtype=jnp.int32)[:, None]
+    thin = unit(high * columns % length, length) + unit(low * columns % length, length)
+    return lax.optimization_barrier(thin)
+
+
+def turned_by(high_real, high_imag, low_real, low_imag):
+    real = high_real * low_real - high_imag * low_imag
+    imag = high_real * low_imag + high_imag * low_real
+    return real, imag
+
+
 def dft_table(length):
-    bins = jnp.arange(length, dtype=jnp.int32)[None, :]
-    high = LOW * jnp.arange(length // LOW, dtype=jnp.int32)[:, None]
-    low = jnp.arange(LOW, dtype=jnp.int32)[:, None]
-    thin = unit(high * bins % length, length) + unit(low * bins % length, length)
-    high_real, high_imag, low_real, low_imag = lax.optimization_barrier(thin)
-    high_real, high_imag = high_real[:, None], high_imag[:, None]
-    real = (high_real * low_real - high_imag * low_imag).astype(jnp.bfloat16)
-    imag = (high_real * low_imag + high_imag * low_real).astype(jnp.bfloat16)
+    thin = thin_tables(length, jnp.arange(length, dtype=jnp.int32), length, LOW)
+    real, imag = turned_by(thin[0][:, None], thin[1][:, None], *thin[2:])
+    real, imag = real.astype(jnp.bfloat16), imag.astype(jnp.bfloat16)
     return real.reshape(length, length), imag.reshape(length, length)
 
 
@@ -106,15 +115,15 @@
     return jnp.where(here, turned[:-1], turned[1:]).reshape(rows, -1)
 
 
-def detect_kernel(last, place_ref, off_ref, low_ref, mid_ref, up_ref, out_ref, wide):
-    segs, rows, length = mid_ref.shape
+def detect_kernel(last, place_ref, off_ref, near_ref, out_ref, wide):
+    segs, rows, length = wide.shape[0], out_ref.shape[1], out_ref.shape[2]
     t = pl.program_id(0)
 
     @pl.when(t == 0)
     def _():
-        wide[:, DMAX : DMAX + rows] = mid_ref[...]
+        wide[:, DMAX : DMAX + rows] = near_ref[:, DMAX : DMAX + rows]
         for s in range(segs):
-            low, up = low_ref[s], up_ref[s]
+            low, up = near_ref[s, :DMAX], near_ref[s, DMAX + rows :]
             wide[s, :DMAX] = jnp.where(place_ref[0] == 0, pltpu.roll(low, 1, 1), low)
             wide[s, DMAX + rows : 2 * DMAX + rows] = jnp.where(
                 place_ref[0] == last, pltpu.roll(up, length - 1, 1), up
@@ -126,31 +135,230 @@
     out_ref[0] = total / segs
 
 
-def detect(fstat, offsets):
-    segs, rows, length = fstat.shape
-    count = lax.axis_size("tm")
-    lower = lax.ppermute(
-        fstat[:, rows - DMAX :], "tm", [(i, (i + 1) % count) for i in range(count)]
-    )
-    upper = lax.ppermute(fstat[:, :DMAX], "tm", [((i + 1) % count, i) for i in range(count)])
+def detect(near, offsets):
+    segs, rows, length = near.shape
+    rows = rows - 2 * DMAX
     place = lax.axis_index("tm").reshape(1)
     templates = offsets.shape[0]
     smem = pl.BlockSpec(memory_space=pltpu.SMEM)
-    rim = pl.BlockSpec((segs, DMAX, length), lambda t: (0, 0, 0))
     return pl.pallas_call(
-        functools.partial(detect_kernel, count - 1),
+        functools.partial(detect_kernel, lax.axis_size("tm") - 1),
         grid=(templates,),
-        in_specs=[smem, smem, rim, pl.BlockSpec(fstat.shape, lambda t: (0, 0, 0)), rim],
+        in_specs=[smem, smem, pl.BlockSpec(near.shape, lambda t: (0, 0, 0))],
         out_specs=pl.BlockSpec((1, rows, length), lambda t: (t, 0, 0)),
         out_shape=jax.ShapeDtypeStruct((templates, rows, length), jnp.float32),
         scratch_shapes=[pltpu.VMEM((segs, rows + 3 * DMAX, length), jnp.float32)],
-    )(place, offsets, lower, fstat, upper)
+    )(place, offsets, near)
+
+
+def with_halo(fstat):
+    rows = fstat.shape[1]
+    count = lax.axis_size("tm")
+    up = [(i, (i + 1) % count) for i in range(count)]
+    lower = lax.ppermute(fstat[:, rows - DMAX :], "tm", up)
+    upper = lax.ppermute(fstat[:, :DMAX], "tm", [(b, a) for a, b in up])
+    return jnp.concatenate([lower, fstat, upper], axis=1)
+
+
+def expand(thin, real_ref, imag_ref):
+    high_real, high_imag, low_real, low_imag = thin
+    step = low_real.shape[0]
+
+    def body(a, carry):
+        real, imag = turned_by(
+            high_real[pl.ds(a, 1), :], high_imag[pl.ds(a, 1), :], low_real[...], low_imag[...]
+        )
+        place = pl.ds(pl.multiple_of(a * step, step), step)
+        real_ref[place, :] = real.astype(real_ref.dtype)
+        imag_ref[place, :] = imag.astype(imag_ref.dtype)
+        return carry
+
+    lax.fori_loop(0, high_real.shape[0], body, 0)
+
+
+def spectrum_kernel(count, *refs):
+    coef, series = refs[:2]
+    thin_turn, thin_short, thin_long = refs[2:6], refs[6:10], refs[10:14]
+    out = refs[14]
+    members, twiddled, arrived, wide = refs[15:19]
+    turn_real, turn_imag, short_real, short_imag, long_real, long_imag = refs[19:25]
+    go_sem, come_sem, back_sem, land_sem, rim_sem, edge_sem = refs[25:]
+    segs, comps, part, length = series.shape
+    rows, width = members.shape[2:]
+    me = lax.axis_index("tm")
+    my_rows = pl.ds(pl.multiple_of(me * part, part), part)
+    my_columns = pl.ds(pl.multiple_of(me * width, width), width)
+    chunks = [(s, lead) for s in range(segs) for lead in range(0, comps, 2)]
+
+    barrier = pltpu.get_barrier_semaphore()
+
+    def greet(step, carry):
+        pl.semaphore_signal(barrier, inc=1, device_id={"tm": lax.rem(me + step, count)})
+        return carry
+
+    lax.fori_loop(1, count, greet, 0)
+    pl.semaphore_wait(barrier, count - 1)
+
+    for q, (s, lead) in enumerate(chunks):
+        pair = pl.ds(lead, 2)
+
+        def send(step, carry):
+            peer = lax.rem(me + step, count)
+            theirs = pl.ds(pl.multiple_of(peer * width, width), width)
+            pltpu.make_async_remote_copy(
+                src_ref=series.at[s, pair, :, theirs],
+                dst_ref=members.at[s, pair, my_rows, :],
+                send_sem=go_sem.at[q],
+                recv_sem=come_sem.at[q],
+                device_id={"tm": peer},
+            ).start()
+            return carry
+
+        lax.fori_loop(1, count, send, 0)
+
+    for s in range(segs):
+        for c in range(comps):
+            members[s, c, my_rows, :] = series[s, c, :, my_columns]
+    expand(thin_turn, turn_real, turn_imag)
+    expand(thin_short, short_real, short_imag)
+
+    def settle(sem, q):
+        some = members.at[0, pl.ds(0, 2), pl.ds(0, (count - 1) * part), :]
+        pltpu.make_async_copy(some, some, sem.at[q]).wait()
+
+    expand(thin_long, long_real, long_imag)
+    tile = math.gcd(256, rows)
+    for q, (s, lead) in enumerate(chunks):
+        settle(come_sem, q)
+        pair = pl.ds(lead, 2)
+        both = jnp.concatenate([members[s, lead], members[s, lead + 1]], axis=-1)
+
+        def strip(r, carry):
+            place = pl.ds(pl.multiple_of(r * tile, tile), tile)
+            by_real = dot(short_real[place, :], both)
+            by_imag = dot(short_imag[place, :], both)
+            real, imag = turned_by(
+                by_real[:, :width] - by_imag[:, width:],
+                by_imag[:, :width] + by_real[:, width:],
+                turn_real[place, :],
+                turn_imag[place, :],
+            )
+            twiddled[s, lead, place, :] = real.astype(jnp.bfloat16)
+            twiddled[s, lead + 1, place, :] = imag.astype(jnp.bfloat16)
+            return carry
+
+        lax.fori_loop(0, rows // tile, strip, 0)
+
+        def send_back(step, carry):
+            peer = lax.rem(me + step, count)
+            theirs = pl.ds(pl.multiple_of(peer * part, part), part)
+            pltpu.make_async_remote_copy(
+                src_ref=twiddled.at[s, pair, theirs, :],
+                dst_ref=arrived.at[s, pair, :, my_columns],
+                send_sem=back_sem.at[q],
+                recv_sem=land_sem.at[q],
+                device_id={"tm": peer},
+            ).start()
+            return carry
+
+        lax.fori_loop(1, count, send_back, 0)
+        for c in (lead, lead + 1):
+            arrived[s, c, :, my_columns] = twiddled[s, c, my_rows, :]
+
+    slab = math.gcd(512, length)
+    rims = []
+    for s in range(segs):
+        for q in range(s * comps // 2, (s + 1) * comps // 2):
+            settle(land_sem, q)
+        a, b, c = coef[s, 0], coef[s, 1], coef[s, 2]
+
+        def project(k, carry):
+            place = pl.ds(pl.multiple_of(k * slab, slab), slab)
+            flat = arrived[s].reshape(comps * part, length)
+            by_real = dot(flat, long_real[:, place]).reshape(comps, part, slab)
+            by_imag = dot(flat, long_imag[:, place]).reshape(comps, part, slab)
+            ar, ai = by_real[0] - by_imag[1], by_imag[0] + by_real[1]
+            br, bi = by_real[2] - by_imag[3], by_imag[2] + by_real[3]
+            numer = (
+                b * (ar * ar + ai * ai) + a * (br * br + bi * bi) - 2.0 * c * (ar * br + ai * bi)
+            )
+            scale = (a * b - c * c) * float(rows * length)
+            wide[s, DMAX : DMAX + part, place] = numer / scale
+            return carry
+
+        lax.fori_loop(0, length // slab, project, 0)
+        for way, (source, target, peer) in enumerate(
+            [
+                (part, 0, lax.rem(me + 1, count)),
+                (DMAX, DMAX + part, lax.rem(me + count - 1, count)),
+            ]
+        ):
+            rim = pltpu.make_async_remote_copy(
+                src_ref=wide.at[s, pl.ds(source, DMAX), :],
+                dst_ref=wide.at[s, pl.ds(target, DMAX), :],
+                send_sem=rim_sem.at[s, way],
+                recv_sem=edge_sem.at[s, way],
+                device_id={"tm": peer},
+            )
+            rim.start()
+            rims.append(rim)
+    for q in range(len(chunks)):
+        settle(go_sem, q)
+        settle(back_sem, q)
+    for rim in rims:
+        rim.wait()
+    out[...] = wide[...]
+
+
+def spectrum(series, antenna, count):
+    segs, comps, part, length = series.shape
+    rows, width = part * count, length // count
+    columns = lax.axis_index("tm") * width + jnp.arange(width, dtype=jnp.int32)
+    thin = (
+        thin_tables(rows * length, columns, rows, 32)
+        + thin_tables(rows, jnp.arange(rows, dtype=jnp.int32), rows, 32)
+        + thin_tables(length, jnp.arange(length, dtype=jnp.int32), length, 32)
+    )
+    vmem = pl.BlockSpec(memory_space=pltpu.VMEM)
+    half = jnp.bfloat16
+    chunks = segs * comps // 2
+    dma = pltpu.SemaphoreType.DMA
+    near = (segs, part + 2 * DMAX, length)
+    return pl.pallas_call(
+        functools.partial(spectrum_kernel, count),
+        in_specs=[pl.BlockSpec(memory_space=pltpu.SMEM)] + [vmem] * (1 + len(thin)),
+        out_specs=vmem,
+        out_shape=jax.ShapeDtypeStruct(near, jnp.float32),
+        scratch_shapes=[
+            pltpu.VMEM((segs, comps, rows, width), half),
+            pltpu.VMEM((segs, comps, rows, width), half),
+            pltpu.VMEM(series.shape, half),
+            pltpu.VMEM(near, jnp.float32),
+            pltpu.VMEM((rows, width), jnp.float32),
+            pltpu.VMEM((rows, width), jnp.float32),
+            pltpu.VMEM((rows, rows), half),
+            pltpu.VMEM((rows, rows), half),
+            pltpu.VMEM((length, length), half),
+            pltpu.VMEM((length, length), half),
+            dma((chunks,)),
+            dma((chunks,)),
+            dma((chunks,)),
+            dma((chunks,)),
+            dma((segs, 2)),
+            dma((segs, 2)),
+        ],
+        compiler_params=pltpu.CompilerParams(
+            collective_id=0, has_side_effects=True, vmem_limit_bytes=60 * 1024 * 1024
+        ),
+    )(antenna, series, *thin)
 
 
 def local(series, antenna, offsets):
     count = lax.axis_size("tm")
     rows, length = series.shape[2] * count, series.shape[3]
     width = length // count
+    if width % 128 == 0 and series.shape[2] % 32 == 0:
+        return detect(spectrum(series, antenna, count), offsets)
     bins = rows * length
     columns = lax.axis_index("tm") * width + jnp.arange(width, dtype=jnp.int32)
     turns = jnp.arange(rows, dtype=jnp.int32)[:, None] * columns[None, :] % bins
@@ -160,7 +368,7 @@
     twiddled = first_stage(members, short, twiddle)
     members = lax.all_to_all(twiddled, "tm", split_axis=2, concat_axis=3, tiled=True)
     fstat = second_stage(members, long, antenna, bins)
-    return detect(fstat, offsets)
+    return detect(with_halo(fstat), offsets)
 
 
 def solution(mesh):

time: 189 us -> 127 us (0.67)
  Pallas kernels: 34.8 us -> 117 us
  waiting for transfers between devices: 64.8 us -> 0 us
  local copies, waits for them, and re-layouts: 40.2 us -> 1.33 us
  starting transfers between devices: 28.6 us -> 0 us
  other arithmetic: 19.1 us -> 8.73 us
    pallas_call x3 -> x2, Pallas kernels: 34.8 us -> 117 us  [the longest x1 112 us: spectrum(): pl.pallas_call(functools.partial(spectrum_kernel, count), in_specs=[pl.Bl...]
    all_to_all x2 -> x0, waiting for transfers between devices: 62.8 us -> none  [the longest x1 33.3 us: local(): lax.all_to_all(series, 'tm', split_axis=3, concat_axis=2, tiled=True)]
    unnamed x10 -> x1, local copies, waits for them, and re-layouts: 20.8 us -> 1.33 us
    all_to_all x2 -> x0, starting transfers between devices: 18.6 us -> none  [the longest x1 11.2 us: local(): lax.all_to_all(twiddled, 'tm', split_axis=2, concat_axis=3, tiled=True)]
    all_to_all x3 -> x0, local copies, waits for them, and re-layouts: 13.8 us -> none  [the longest x1 6.97 us: local(): lax.all_to_all(series, 'tm', split_axis=3, concat_axis=2, tiled=True)]
    convert_element_type x2 -> x0, other arithmetic: 11.5 us -> none  [dft_table(): imag = (high_real * low_imag + high_imag * low_real).astype(jnp.bfloat16)]
    ppermute x2 -> x0, starting transfers between devices: 9.95 us -> none  [the longest x1 8.93 us: detect(): lax.ppermute(fstat[:, :DMAX], 'tm', [((i + 1) % count, i) for i in range(...]
    pallas_call x1 -> x0, local copies, waits for them, and re-layouts: 4.54 us -> none  [first_stage(): pl.pallas_call(first_kernel, grid=(segs, comps // 2, rows // tile), in_sp...]
  transfers between devices with their start and end apart: 4 -> 0, of which waited for: 3 -> 0; matrix products, arithmetic and copies ran while one was open for 11% -> 0% of each run, Pallas kernels for 0% -> 0%
where the time goes in v2:
time: 127 us
  Pallas kernels  117 us (92%)
  other arithmetic  8.73 us (7%)
  local copies, waits for them, and re-layouts  1.33 us (1%)
    pallas_call x1, Pallas kernels, spectrum(): pl.pallas_call(functools.partial(spectrum_kernel, count), in_specs=[pl.Bl...  112 us
    neg x4, other arithmetic, unit(): return (jnp.cos(angle), -jnp.sin(angle))  7.57 us
    pallas_call x1, Pallas kernels, detect(): pl.pallas_call(functools.partial(detect_kernel, lax.axis_size('tm') - 1),...  5.34 us

profile of v2, /device:TPU:0, one launch (start us, length us, event | category | flops | bytes accessed | tf_op | source)
XLA Modules:
  0.0 127.3 jit_solution(17576602239434134856)
XLA Ops:
  0.0 1.3 %copy.4.off_ref = s32[8,2]{1,0:T(8,128)} copy(s32[8,2]{0,1:T(2,128)} %param.5) | data formatting | bytes 128 | tf_op args[2]
  1.3 0.8 sine_negate_fusion.5
  2.1 1.1 fusion.26.refs_8_
  3.3 1.8 %sine_negate_fusion.3 = (f32[32,1024]{1,0:T(8,128)}, f32[32,1024]{1,0:T(8,128)}, f32[32,1024]{1,0:T(8,128)}) fusion(s32[32]{0:T(128)S(1)} %iota_multiply_fusion.1), kind=kLoop, calls=%fused_computation.37 | loop fusion | flops 983040 | bytes 393344 | tf_op jit(solution)/shard_map/neg | solution.py:17
  5.1 1.8 %sine_negate_fusion.1 = (f32[32,2048]{1,0:T(8,128)}, f32[32,2048]{1,0:T(8,128)}) fusion(), kind=kLoop, calls=%fused_computation.16 | loop fusion | flops 983040 | bytes 524288 | tf_op jit(solution)/shard_map/neg | solution.py:17
  6.8 3.2 %sine_negate_fusion = (f32[64,2048]{1,0:T(8,128)}, f32[64,2048]{1,0:T(8,128)}) fusion(s32[64]{0:T(128)S(1)} %iota_multiply_fusion), kind=kLoop, calls=%fused_computation.6 | loop fusion | flops 1966080 | bytes 1048832 | tf_op jit(solution)/shard_map/neg | solution.py:17
  10.1 111.9 %shard_map.37.near_ref = f32[2,80,2048]{2,1,0:T(8,128)} custom-call(f32[2,3]{1,0:T(2,128)} %refs_0_.1, bf16[2,4,64,2048]{3,2,1,0:T(8,128)(2,1)} %refs_1_.1, f32[32,128]{1,0:T(8,128)} %get-tuple-element.17.refs_2_, f32[32,128]{1,0:T(8,128)} %get-tuple-element.18.refs_3_, f32[32,128]{1,0:T(8,128)} %get-tuple-element.19.refs_4_, ...), custom_call_target="tpu_custom_call" | custom-call | tf_op jit(solution)/shard_map/pallas_call | solution.py:327
  121.9 5.3 %shard_map.38 = f32[8,64,2048]{2,1,0:T(8,128)} custom-call(s32[1]{0:T(128)} %bitcast.place_ref, s32[8,2]{1,0:T(8,128)} %copy.4.off_ref, f32[2,80,2048]{2,1,0:T(8,128)} %shard_map.37.near_ref), custom_call_target="tpu_custom_call" | custom-call | tf_op jit(solution)/shard_map/pallas_call | solution.py:144
  (3 shorter events, 0.0 us)

commit v3 on v2

--- a/solution.py
+++ b/solution.py
@@ -129,9 +129,9 @@
                 place_ref[0] == last, pltpu.roll(up, length - 1, 1), up
             )
 
-    total = shifted(wide, 0, DMAX + off_ref[t, 0], rows)
+    total = shifted(wide, 0, DMAX + off_ref[0, t], rows)
     for s in range(1, segs):
-        total = total + shifted(wide, s, DMAX + off_ref[t, s], rows)
+        total = total + shifted(wide, s, DMAX + off_ref[s, t], rows)
     out_ref[0] = total / segs
 
 
@@ -148,7 +148,7 @@
         out_specs=pl.BlockSpec((1, rows, length), lambda t: (t, 0, 0)),
         out_shape=jax.ShapeDtypeStruct((templates, rows, length), jnp.float32),
         scratch_shapes=[pltpu.VMEM((segs, rows + 3 * DMAX, length), jnp.float32)],
-    )(place, offsets, near)
+    )(place, offsets.T, near)
 
 
 def with_halo(fstat):
@@ -160,9 +160,13 @@
     return jnp.concatenate([lower, fstat, upper], axis=1)
 
 
-def expand(thin, real_ref, imag_ref):
+def expand(length, first, thin, real_ref, imag_ref):
     high_real, high_imag, low_real, low_imag = thin
     step = low_real.shape[0]
+    for scale, real, imag in ((step, high_real, high_imag), (1, low_real, low_imag)):
+        rows = scale * lax.broadcasted_iota(jnp.int32, real.shape, 0)
+        columns = first + lax.broadcasted_iota(jnp.int32, real.shape, 1)
+        real[...], imag[...] = unit(lax.rem(rows * columns, jnp.full_like(rows, length)), length)
 
     def body(a, carry):
         real, imag = turned_by(
@@ -177,12 +181,11 @@
 
 
 def spectrum_kernel(count, *refs):
-    coef, series = refs[:2]
-    thin_turn, thin_short, thin_long = refs[2:6], refs[6:10], refs[10:14]
-    out = refs[14]
-    members, twiddled, arrived, wide = refs[15:19]
-    turn_real, turn_imag, short_real, short_imag, long_real, long_imag = refs[19:25]
-    go_sem, come_sem, back_sem, land_sem, rim_sem, edge_sem = refs[25:]
+    coef, series, out = refs[:3]
+    members, twiddled, arrived, wide = refs[3:7]
+    turn_real, turn_imag, short_real, short_imag, long_real, long_imag = refs[7:13]
+    go_sem, come_sem, back_sem, land_sem, rim_sem, edge_sem = refs[13:19]
+    thin_turn, thin_short, thin_long = refs[19:23], refs[23:27], refs[27:31]
     segs, comps, part, length = series.shape
     rows, width = members.shape[2:]
     me = lax.axis_index("tm")
@@ -196,14 +199,27 @@
         pl.semaphore_signal(barrier, inc=1, device_id={"tm": lax.rem(me + step, count)})
         return carry
 
+    def to_each(start):
+        if count % 2:
+            return lax.fori_loop(1, count, lambda n, c: start(lax.rem(me + n, count), c), 0)
+        mid = count // 2
+        side, seat = me // mid, lax.rem(me, mid)
+
+        def body(n, carry):
+            turn = lax.rem(seat + n, mid)
+            start(side * mid + turn, carry)
+            return start((1 - side) * mid + turn, carry)
+
+        start((1 - side) * mid + seat, 0)
+        return lax.fori_loop(1, mid, body, 0)
+
     lax.fori_loop(1, count, greet, 0)
     pl.semaphore_wait(barrier, count - 1)
 
     for q, (s, lead) in enumerate(chunks):
         pair = pl.ds(lead, 2)
 
-        def send(step, carry):
-            peer = lax.rem(me + step, count)
+        def send(peer, carry):
             theirs = pl.ds(pl.multiple_of(peer * width, width), width)
             pltpu.make_async_remote_copy(
                 src_ref=series.at[s, pair, :, theirs],
@@ -214,19 +230,18 @@
             ).start()
             return carry
 
-        lax.fori_loop(1, count, send, 0)
+        to_each(send)
 
     for s in range(segs):
         for c in range(comps):
             members[s, c, my_rows, :] = series[s, c, :, my_columns]
-    expand(thin_turn, turn_real, turn_imag)
-    expand(thin_short, short_real, short_imag)
+    expand(rows * length, me * width, thin_turn, turn_real, turn_imag)
+    expand(rows, 0, thin_short, short_real, short_imag)
 
     def settle(sem, q):
         some = members.at[0, pl.ds(0, 2), pl.ds(0, (count - 1) * part), :]
         pltpu.make_async_copy(some, some, sem.at[q]).wait()
 
-    expand(thin_long, long_real, long_imag)
     tile = math.gcd(256, rows)
     for q, (s, lead) in enumerate(chunks):
         settle(come_sem, q)
@@ -249,8 +264,7 @@
 
         lax.fori_loop(0, rows // tile, strip, 0)
 
-        def send_back(step, carry):
-            peer = lax.rem(me + step, count)
+        def send_back(peer, carry):
             theirs = pl.ds(pl.multiple_of(peer * part, part), part)
             pltpu.make_async_remote_copy(
                 src_ref=twiddled.at[s, pair, theirs, :],
@@ -261,9 +275,11 @@
             ).start()
             return carry
 
-        lax.fori_loop(1, count, send_back, 0)
+        to_each(send_back)
         for c in (lead, lead + 1):
             arrived[s, c, :, my_columns] = twiddled[s, c, my_rows, :]
+        if q == 0:
+            expand(length, 0, thin_long, long_real, long_imag)
 
     slab = math.gcd(512, length)
     rims = []
@@ -313,20 +329,18 @@
 def spectrum(series, antenna, count):
     segs, comps, part, length = series.shape
     rows, width = part * count, length // count
-    columns = lax.axis_index("tm") * width + jnp.arange(width, dtype=jnp.int32)
-    thin = (
-        thin_tables(rows * length, columns, rows, 32)
-        + thin_tables(rows, jnp.arange(rows, dtype=jnp.int32), rows, 32)
-        + thin_tables(length, jnp.arange(length, dtype=jnp.int32), length, 32)
-    )
     vmem = pl.BlockSpec(memory_space=pltpu.VMEM)
     half = jnp.bfloat16
+
+    def thin(tall, across):
+        return [pltpu.VMEM((n, across), jnp.float32) for n in (tall // 32, tall // 32, 32, 32)]
+
     chunks = segs * comps // 2
     dma = pltpu.SemaphoreType.DMA
     near = (segs, part + 2 * DMAX, length)
     return pl.pallas_call(
         functools.partial(spectrum_kernel, count),
-        in_specs=[pl.BlockSpec(memory_space=pltpu.SMEM)] + [vmem] * (1 + len(thin)),
+        in_specs=[pl.BlockSpec(memory_space=pltpu.SMEM)] + [vmem],
         out_specs=vmem,
         out_shape=jax.ShapeDtypeStruct(near, jnp.float32),
         scratch_shapes=[
@@ -346,11 +360,14 @@
             dma((chunks,)),
             dma((segs, 2)),
             dma((segs, 2)),
-        ],
+        ]
+        + thin(rows, width)
+        + thin(rows, rows)
+        + thin(length, length),
         compiler_params=pltpu.CompilerParams(
             collective_id=0, has_side_effects=True, vmem_limit_bytes=60 * 1024 * 1024
         ),
-    )(antenna, series, *thin)
+    )(antenna, series)
 
 
 def local(series, antenna, offsets):

time: 127 us -> 114 us (0.90)
  other arithmetic: 8.73 us -> 0 us
  Pallas kernels: 117 us -> 114 us
  local copies, waits for them, and re-layouts: 1.33 us -> 0 us
    neg x4 -> x0, other arithmetic: 7.57 us -> none  [unit(): return (jnp.cos(angle), -jnp.sin(angle))]
    pallas_call x1, Pallas kernels: 112 us -> 109 us  [spectrum(): pl.pallas_call(functools.partial(spectrum_kernel, count), in_specs=[pl.Bl...]
    unnamed x1 -> x0, local copies, waits for them, and re-layouts: 1.33 us -> none
where the time goes in v3:
time: 114 us
  Pallas kernels  114 us (100%)
    pallas_call x1, Pallas kernels, spectrum(): pl.pallas_call(functools.partial(spectrum_kernel, count), in_specs=[pl.Bl...  109 us
    pallas_call x1, Pallas kernels, detect(): pl.pallas_call(functools.partial(detect_kernel, lax.axis_size('tm') - 1),...  5.33 us

profile of v3, /device:TPU:0, one launch (start us, length us, event | category | flops | bytes accessed | tf_op | source)
XLA Modules:
  0.0 114.2 jit_solution(16541530453739319686)
XLA Ops:
  0.0 108.9 %shard_map.37.near_ref = f32[2,80,2048]{2,1,0:T(8,128)} custom-call(f32[2,3]{1,0:T(2,128)} %refs_0_.1, bf16[2,4,64,2048]{3,2,1,0:T(8,128)(2,1)} %refs_1_.1), custom_call_target="tpu_custom_call" | custom-call | tf_op jit(solution)/shard_map/pallas_call | solution.py:341
  108.9 5.3 %shard_map.38 = f32[8,64,2048]{2,1,0:T(8,128)} custom-call(s32[1]{0:T(128)} %bitcast.place_ref, s32[2,8]{1,0:T(2,128)} %bitcast.2, f32[2,80,2048]{2,1,0:T(8,128)} %shard_map.37.near_ref), custom_call_target="tpu_custom_call" | custom-call | tf_op jit(solution)/shard_map/pallas_call | solution.py:144

commit v4 on v3

--- a/solution.py
+++ b/solution.py
@@ -181,11 +181,12 @@
 
 
 def spectrum_kernel(count, *refs):
-    coef, series, out = refs[:3]
+    coef, given, out = refs[:3]
     members, twiddled, arrived, wide = refs[3:7]
     turn_real, turn_imag, short_real, short_imag, long_real, long_imag = refs[7:13]
     go_sem, come_sem, back_sem, land_sem, rim_sem, edge_sem = refs[13:19]
     thin_turn, thin_short, thin_long = refs[19:23], refs[23:27], refs[27:31]
+    series, field, load_sem = refs[31:]
     segs, comps, part, length = series.shape
     rows, width = members.shape[2:]
     me = lax.axis_index("tm")
@@ -193,6 +194,8 @@
     my_columns = pl.ds(pl.multiple_of(me * width, width), width)
     chunks = [(s, lead) for s in range(segs) for lead in range(0, comps, 2)]
 
+    load = pltpu.make_async_copy(given, series, load_sem)
+    load.start()
     barrier = pltpu.get_barrier_semaphore()
 
     def greet(step, carry):
@@ -215,6 +218,7 @@
 
     lax.fori_loop(1, count, greet, 0)
     pl.semaphore_wait(barrier, count - 1)
+    load.wait()
 
     for q, (s, lead) in enumerate(chunks):
         pair = pl.ds(lead, 2)
@@ -283,18 +287,22 @@
 
     slab = math.gcd(512, length)
     rims = []
-    for s in range(segs):
-        for q in range(s * comps // 2, (s + 1) * comps // 2):
-            settle(land_sem, q)
+    last = comps - 2
+    for q, (s, lead) in enumerate(chunks):
+        settle(land_sem, q)
         a, b, c = coef[s, 0], coef[s, 1], coef[s, 2]
 
         def project(k, carry):
             place = pl.ds(pl.multiple_of(k * slab, slab), slab)
-            flat = arrived[s].reshape(comps * part, length)
-            by_real = dot(flat, long_real[:, place]).reshape(comps, part, slab)
-            by_imag = dot(flat, long_imag[:, place]).reshape(comps, part, slab)
-            ar, ai = by_real[0] - by_imag[1], by_imag[0] + by_real[1]
-            br, bi = by_real[2] - by_imag[3], by_imag[2] + by_real[3]
+            flat = arrived[s, lead : lead + 2].reshape(2 * part, length)
+            by_real = dot(flat, long_real[:, place])
+            by_imag = dot(flat, long_imag[:, place])
+            real, imag = by_real[:part] - by_imag[part:], by_imag[:part] + by_real[part:]
+            if lead != last:
+                field[0, :, place] = real
+                field[1, :, place] = imag
+                return carry
+            ar, ai, br, bi = field[0, :, place], field[1, :, place], real, imag
             numer = (
                 b * (ar * ar + ai * ai) + a * (br * br + bi * bi) - 2.0 * c * (ar * br + ai * bi)
             )
@@ -303,6 +311,8 @@
             return carry
 
         lax.fori_loop(0, length // slab, project, 0)
+        if lead != last:
+            continue
         for way, (source, target, peer) in enumerate(
             [
                 (part, 0, lax.rem(me + 1, count)),
@@ -321,9 +331,12 @@
     for q in range(len(chunks)):
         settle(go_sem, q)
         settle(back_sem, q)
+    own = slice(DMAX, DMAX + part)
+    out[:, own] = wide[:, own]
     for rim in rims:
         rim.wait()
-    out[...] = wide[...]
+    out[:, :DMAX] = wide[:, :DMAX]
+    out[:, DMAX + part :] = wide[:, DMAX + part :]
 
 
 def spectrum(series, antenna, count):
@@ -340,7 +353,7 @@
     near = (segs, part + 2 * DMAX, length)
     return pl.pallas_call(
         functools.partial(spectrum_kernel, count),
-        in_specs=[pl.BlockSpec(memory_space=pltpu.SMEM)] + [vmem],
+        in_specs=[pl.BlockSpec(memory_space=pltpu.SMEM), pl.BlockSpec(memory_space=pl.ANY)],
         out_specs=vmem,
         out_shape=jax.ShapeDtypeStruct(near, jnp.float32),
         scratch_shapes=[
@@ -363,7 +376,12 @@
         ]
         + thin(rows, width)
         + thin(rows, rows)
-        + thin(length, length),
+        + thin(length, length)
+        + [
+            pltpu.VMEM(series.shape, half),
+            pltpu.VMEM((2, part, length), jnp.float32),
+            dma,
+        ],
         compiler_params=pltpu.CompilerParams(
             collective_id=0, has_side_effects=True, vmem_limit_bytes=60 * 1024 * 1024
         ),

time: 114 us -> 111 us (0.974)
  Pallas kernels: 114 us -> 111 us
    pallas_call x1, Pallas kernels: 109 us -> 106 us  [spectrum(): pl.pallas_call(functools.partial(spectrum_kernel, count), in_specs=[pl.Bl...]
where the time goes in v4:
time: 111 us
  Pallas kernels  111 us (100%)
    pallas_call x1, Pallas kernels, spectrum(): pl.pallas_call(functools.partial(spectrum_kernel, count), in_specs=[pl.Bl...  106 us
    pallas_call x1, Pallas kernels, detect(): pl.pallas_call(functools.partial(detect_kernel, lax.axis_size('tm') - 1),...  5.33 us

profile of v4, /device:TPU:0, one launch (start us, length us, event | category | flops | bytes accessed | tf_op | source)
XLA Modules:
  0.0 111.2 jit_solution(14596401446834803940)
XLA Ops:
  0.0 105.8 %shard_map.37.near_ref = f32[2,80,2048]{2,1,0:T(8,128)} custom-call(f32[2,3]{1,0:T(2,128)} %refs_0_.1, bf16[2,4,64,2048]{3,2,1,0:T(8,128)(2,1)} %refs_1_.1), custom_call_target="tpu_custom_call" | custom-call | tf_op jit(solution)/shard_map/pallas_call | solution.py:354
  105.8 5.3 %shard_map.38 = f32[8,64,2048]{2,1,0:T(8,128)} custom-call(s32[1]{0:T(128)} %bitcast.place_ref, s32[2,8]{1,0:T(2,128)} %bitcast.2, f32[2,80,2048]{2,1,0:T(8,128)} %shard_map.37.near_ref), custom_call_target="tpu_custom_call" | custom-call | tf_op jit(solution)/shard_map/pallas_call | solution.py:144

commit v5 on v4

--- a/solution.py
+++ b/solution.py
@@ -129,10 +129,12 @@
                 place_ref[0] == last, pltpu.roll(up, length - 1, 1), up
             )
 
-    total = shifted(wide, 0, DMAX + off_ref[0, t], rows)
-    for s in range(1, segs):
-        total = total + shifted(wide, s, DMAX + off_ref[s, t], rows)
-    out_ref[0] = total / segs
+    batch = out_ref.shape[0]
+    for i in range(batch):
+        total = shifted(wide, 0, DMAX + off_ref[0, t * batch + i], rows)
+        for s in range(1, segs):
+            total = total + shifted(wide, s, DMAX + off_ref[s, t * batch + i], rows)
+        out_ref[i] = total / segs
 
 
 def detect(near, offsets):
@@ -140,12 +142,13 @@
     rows = rows - 2 * DMAX
     place = lax.axis_index("tm").reshape(1)
     templates = offsets.shape[0]
+    batch = math.gcd(2, templates)
     smem = pl.BlockSpec(memory_space=pltpu.SMEM)
     return pl.pallas_call(
         functools.partial(detect_kernel, lax.axis_size("tm") - 1),
-        grid=(templates,),
+        grid=(templates // batch,),
         in_specs=[smem, smem, pl.BlockSpec(near.shape, lambda t: (0, 0, 0))],
-        out_specs=pl.BlockSpec((1, rows, length), lambda t: (t, 0, 0)),
+        out_specs=pl.BlockSpec((batch, rows, length), lambda t: (t, 0, 0)),
         out_shape=jax.ShapeDtypeStruct((templates, rows, length), jnp.float32),
         scratch_shapes=[pltpu.VMEM((segs, rows + 3 * DMAX, length), jnp.float32)],
     )(place, offsets.T, near)
@@ -310,7 +313,7 @@
             wide[s, DMAX : DMAX + part, place] = numer / scale
             return carry
 
-        lax.fori_loop(0, length // slab, project, 0)
+        lax.fori_loop(0, length // slab, project, 0, unroll=2)
         if lead != last:
             continue
         for way, (source, target, peer) in enumerate(

time: 111 us -> 110 us (level)
  no operation moved by 1% of the time
where the time goes in v5:
time: 110 us
  Pallas kernels  110 us (100%)
    pallas_call x1, Pallas kernels, spectrum(): pl.pallas_call(functools.partial(spectrum_kernel, count), in_specs=[pl.Bl...  106 us
    pallas_call x1, Pallas kernels, detect(): pl.pallas_call(functools.partial(detect_kernel, lax.axis_size('tm') - 1),...  4.23 us

profile of v5, /device:TPU:0, one launch (start us, length us, event | category | flops | bytes accessed | tf_op | source)
XLA Modules:
  0.0 109.7 jit_solution(1154493422736300389)
XLA Ops:
  0.0 105.5 %shard_map.37.near_ref = f32[2,80,2048]{2,1,0:T(8,128)} custom-call(f32[2,3]{1,0:T(2,128)} %refs_0_.1, bf16[2,4,64,2048]{3,2,1,0:T(8,128)(2,1)} %refs_1_.1), custom_call_target="tpu_custom_call" | custom-call | tf_op jit(solution)/shard_map/pallas_call | solution.py:357
  105.5 4.2 %shard_map.38 = f32[8,64,2048]{2,1,0:T(8,128)} custom-call(s32[1]{0:T(128)} %bitcast.place_ref, s32[2,8]{1,0:T(2,128)} %bitcast.2, f32[2,80,2048]{2,1,0:T(8,128)} %shard_map.37.near_ref), custom_call_target="tpu_custom_call" | custom-call | tf_op jit(solution)/shard_map/pallas_call | solution.py:147
